TPU v7x, 512 devices: a whole 4x4x16 slice. The times are simulated.
512 devices in a mesh: leaf: 32 (over x, z_lo, core), col: 16 (over y, z_hi).
Axes of the slice: x: 4, y: 4, z: 16 (z_hi: 4, z_lo: 4; z = z_hi * 4 + z_lo), core: 2. Of those that a mesh axis runs over, the one named last changes fastest.
Arguments:
- right_sides: float32 [256, 65536], P('col', 'leaf'), may hold values from -6 to 6
- inverse_first: float32 [128, 128, 128], P('leaf'), may hold values from -0.5 to 0.5
- coupling_first: float32 [128, 3, 128, 128], P('leaf'), may hold values from -0.3125 to 0.3125
- links_first: int32 [128, 3], P('leaf'), may hold values from 0 to 11, as said below
- order_first: int32 [32, 12], P('leaf'), may hold values from 0 to 11, as said below
- inverse_second: float32 [128, 128, 128], P('leaf'), may hold values from -0.5 to 0.5
- coupling_second: float32 [128, 3, 128, 128], P('leaf'), may hold values from -0.3125 to 0.3125
- links_second: int32 [128, 3], P('leaf'), may hold values from 0 to 7, as said below
- order_second: int32 [32, 8], P('leaf'), may hold values from 0 to 7, as said below
- inverse_third: float32 [128, 128, 128], P('leaf'), may hold values from -0.5 to 0.5
- coupling_third: float32 [128, 3, 128, 128], P('leaf'), may hold values from -0.3125 to 0.3125
- links_third: int32 [128, 3], P('leaf'), may hold values from 0 to 3, as said below
- order_third: int32 [32, 4], P('leaf'), may hold values from 0 to 3, as said below
- front_rows: int32 [3, 32], P(None, 'leaf'), may hold values from 128 to 512
- root_inverse: float32 [2, 8192, 8192], P(None, 'leaf', 'col'), may hold values from -0.0625 to 0.0625
- root_coupling: float32 [8192, 8192], P('leaf', 'col'), may hold values from -0.0625 to 0.0625
Outputs:
- solved_first: float32 [256, 16384], P('col', 'leaf')
- solved_second: float32 [256, 16384], P('col', 'leaf')
- solved_third: float32 [256, 16384], P('col', 'leaf')
- root_solution: float32 [256, 2, 8192], P('col', None, 'leaf')
Inputs may be any that keep to these rules, and one draw needn't show every extreme that they name: `links_first`: each row names 3 different skeleton blocks of its front. `links_second`: each row names 3 different skeleton blocks of its front. `links_third`: each row names 3 different skeleton blocks of its front. `order_first`: each row is a permutation. `order_second`: each row is a permutation. `order_third`: each row is a permutation.
All inputs are finite; a program needn't handle non-finite values.
Results may differ from a plain program's by a relative error of at most 0.0003.
Values sent between devices are 32-bit elements; how exact they have to be, the bound alone decides.
A program may use at most 64 MiB of HBM per device.

v0:
```python
import jax
import jax.numpy as jnp
from jax import lax
from jax.sharding import PartitionSpec as P


def partner(block, axis, stride):
    count = lax.axis_size(axis)
    route = []
    for low in range(count):
        high = low | 1 << stride
        if high != low and high < count:
            route += [(low, high), (high, low)]
    return lax.ppermute(block, axis, route)


def eliminate(section, inverse, coupling, link_ids, live_count):
    block_rows = inverse.shape[-1]
    red_blocks = inverse.shape[0]
    link_total = coupling.shape[1]
    rhs_rows = section.shape[0]
    skeleton_count = section.shape[1] // block_rows - red_blocks
    redundant = section[:, : red_blocks * block_rows].reshape(rhs_rows, red_blocks, block_rows)
    positions = lax.broadcasted_iota(
        jnp.int32, (red_blocks, block_rows), 0
    ) * block_rows + lax.broadcasted_iota(jnp.int32, (red_blocks, block_rows), 1)
    live_rows = (positions < live_count).astype(jnp.float32)
    solved = (
        jnp.einsum("rib,iba->ria", redundant * live_rows, inverse, precision=lax.Precision.HIGHEST)
        * live_rows
    )
    pushed = jnp.einsum("ria,ikab->rikb", solved, coupling, precision=lax.Precision.HIGHEST)
    targets = (
        link_ids[:, :, None]
        == lax.broadcasted_iota(jnp.int32, (red_blocks, link_total, skeleton_count), 2)
    ).astype(jnp.float32)
    update = jnp.einsum("rikb,iks->rsb", pushed, targets, precision=lax.Precision.HIGHEST)
    skeleton = (
        section[:, red_blocks * block_rows :].reshape(rhs_rows, skeleton_count, block_rows) - update
    )
    return (solved.reshape(rhs_rows, red_blocks * block_rows), skeleton)


def join_halves(skeleton, level_index):
    half_blocks = skeleton.shape[1] // 2
    upper_half = lax.axis_index("leaf") >> level_index & 1
    kept_half = lax.dynamic_slice_in_dim(skeleton, upper_half * half_blocks, half_blocks, 1)
    sent_half = lax.dynamic_slice_in_dim(skeleton, (1 - upper_half) * half_blocks, half_blocks, 1)
    received = partner(sent_half, "leaf", level_index)
    return jnp.where(
        upper_half == 0,
        jnp.concatenate([kept_half, received], 1),
        jnp.concatenate([received, kept_half], 1),
    )


def spread_columns(values):
    return lax.all_gather(values, "col", axis=0, tiled=True)


def spread_leaf(values):
    return lax.all_gather(values, "leaf", axis=0, tiled=True)


def to_leaf_rows(values):
    full_rows = lax.all_gather(values, "col", axis=1, tiled=True)
    return lax.all_to_all(full_rows, "leaf", split_axis=1, concat_axis=0, tiled=True)


def to_column_rows(values):
    full_rows = lax.all_gather(values, "leaf", axis=1, tiled=True)
    return lax.all_to_all(full_rows, "col", split_axis=1, concat_axis=0, tiled=True)


def forward_product(values, matrix):
    return lax.psum_scatter(
        jnp.dot(
            values, matrix, precision=lax.Precision.HIGHEST, preferred_element_type=jnp.float32
        ),
        "leaf",
        scatter_dimension=0,
        tiled=True,
    )


def backward_product(values, matrix):
    return lax.psum_scatter(
        lax.dot_general(
            values,
            matrix,
            (((1,), (1,)), ((), ())),
            precision=lax.Precision.HIGHEST,
            preferred_element_type=jnp.float32,
        ),
        "col",
        scatter_dimension=0,
        tiled=True,
    )


def local(
    right_sides,
    inverse_first,
    coupling_first,
    links_first,
    order_first,
    inverse_second,
    coupling_second,
    links_second,
    order_second,
    inverse_third,
    coupling_third,
    links_third,
    order_third,
    front_rows,
    root_inverse,
    root_coupling,
):
    level_data = (
        (inverse_first, coupling_first, links_first, order_first),
        (inverse_second, coupling_second, links_second, order_second),
        (inverse_third, coupling_third, links_third, order_third),
    )
    section = right_sides
    outputs = []
    for level_index in range(3):
        inverse, coupling, link_ids, order_map = level_data[level_index]
        solved, skeleton = eliminate(
            section, inverse, coupling, link_ids, front_rows[level_index, 0]
        )
        outputs.append(solved)
        if level_index < 2:
            skeleton = join_halves(skeleton, level_index)
        skeleton = jnp.take(skeleton, order_map[0], axis=1)
        section = skeleton.reshape(skeleton.shape[0], -1)
    rhs_rows = right_sides.shape[0]
    panel_count = root_inverse.shape[0]
    panel_rows = root_inverse.shape[1]
    root_rhs = section.reshape(rhs_rows, panel_count, panel_rows)
    full_rhs = spread_columns(root_rhs)
    first_solve = forward_product(full_rhs[:, 0], root_inverse[0])
    coupled = forward_product(to_leaf_rows(first_solve), root_coupling)
    second_solve = forward_product(full_rhs[:, 1] - to_leaf_rows(coupled), root_inverse[1])
    forward_both = spread_leaf(jnp.stack([first_solve, second_solve], 1))
    last_panel = backward_product(forward_both[:, 1], root_inverse[1])
    back_coupled = backward_product(to_column_rows(last_panel), root_coupling)
    first_panel = backward_product(
        forward_both[:, 0] - to_column_rows(back_coupled), root_inverse[0]
    )
    root_solution = jnp.stack([first_panel, last_panel], 1)
    return (outputs[0], outputs[1], outputs[2], root_solution)


def solution(mesh):
    in_specs = (
        P("col", "leaf"),
        P("leaf", None, None),
        P("leaf", None, None, None),
        P("leaf", None),
        P("leaf", None),
        P("leaf", None, None),
        P("leaf", None, None, None),
        P("leaf", None),
        P("leaf", None),
        P("leaf", None, None),
        P("leaf", None, None, None),
        P("leaf", None),
        P("leaf", None),
        P(None, "leaf"),
        P(None, "leaf", "col"),
        P("leaf", "col"),
    )
    out_specs = (P("col", "leaf"), P("col", "leaf"), P("col", "leaf"), P("col", None, "leaf"))
    return jax.shard_map(local, mesh=mesh, in_specs=in_specs, out_specs=out_specs, check_vma=False)
```

profile of v0, /device:TPU:2, one launch (start us, length us, event | category | flops | bytes accessed | tf_op | source)
XLA Modules:
  0.0 1212.6 jit_solution(16037484874511490501)
XLA Ops:
  7.3 0.7 copy-done.11
  8.0 0.6 fusion.52
  8.5 0.1 copy.65
  8.6 0.9 slice-done
  9.6 2.0 fusion.47
  11.6 1.3 convolution_multiply_fusion.2
  12.9 0.6 convolution_bitcast_fusion.3
  13.5 0.3 fusion
  13.9 1.9 collective-permute-start
  15.8 0.6 copy-done.16
  16.5 0.6 copy-done.17
  17.1 0.5 broadcast.169
  17.6 0.7 reduce.3
  18.3 0.1 squeeze.47
  18.4 0.1 broadcast_bitcast_fusion.1
  18.5 0.1 broadcast_bitcast_fusion.2
  18.6 0.1 broadcast_bitcast_fusion
  18.7 0.7 copy-done.13
  19.3 0.1 copy.71
  19.5 0.6 gather_fusion
  20.2 0.8 copy-done.7
  21.1 0.3 convolution_multiply_fusion.1
  21.4 0.6 convolution_bitcast_fusion.2
  22.0 0.3 fusion.1
  22.4 3.8 collective-permute-start.1
  26.2 0.1 copy.77
  26.3 1.9 collective-permute-done.1
  28.3 0.6 gather_fusion.1
  29.0 0.8 copy-done.8
  29.8 0.3 convolution_multiply_fusion
  30.1 0.6 convolution_bitcast_fusion.1
  30.7 0.3 fusion.2
  31.0 0.6 gather_fusion.2
  31.6 62.8 %all_gather.18 = f32[256,2,256]{2,1,0:T(2,128)S(1)} all-gather(f32[16,2,256]{2,1,0:T(2,128)S(1)} %broadcast_select_fusion), channel_id=1, replica_groups=mesh['leaf'=32,'col'=16] {'col'}, dimensions={0}, use_global_device_ids=true | all-gather | bytes 557056 | tf_op jit(solution)/shard_map/all_gather | solution.py:58
  94.5 0.2 slice.72
  94.7 1.4 fusion.11
  96.2 123.1 %reduce-scatter.7.cloned.1.call-done = f32[8,512]{1,0:T(8,128)} async-done(((f32[256,512]{1,0:T(8,128)}), f32[8,512]{1,0:T(8,128)}) %reduce-scatter.7.cloned.1.call-update) | async-done | bytes 16400 | tf_op jit(solution)/shard_map/reduce_scatter | solution.py:76
  219.2 53.1 %all_gather.19 = f32[8,8192]{1,0:T(8,128)S(1)} all-gather(f32[8,512]{1,0:T(8,128)} %reduce-scatter.7.cloned.1.call-done), channel_id=1, replica_groups=mesh['leaf'=32,'col'=16] {'col'}, dimensions={1}, use_global_device_ids=true | all-gather | bytes 278528 | tf_op jit(solution)/shard_map/all_gather | solution.py:66
  272.4 32.4 %all_to_all.76 = f32[8,32,256]{2,0,1:T(8,128)S(1)} all-to-all(f32[8,32,256]{2,0,1:T(8,128)S(1)} %bitcast.194), channel_id=1, replica_groups=mesh['leaf'=32,'col'=16] {'leaf'}, dimensions={1} | all-to-all | bytes 524288 | tf_op jit(solution)/shard_map/all_to_all | solution.py:67
  304.8 1.4 fusion.21
  306.3 0.0 reduce-scatter.11.cloned.1.call-start
  306.3 121.1 %reduce-scatter.9.cloned.1.call-done = f32[8,512]{1,0:T(8,128)} async-done(((f32[256,512]{1,0:T(8,128)}), f32[8,512]{1,0:T(8,128)}) %reduce-scatter.9.cloned.1.call-update) | async-done | bytes 16400 | tf_op jit(solution)/shard_map/reduce_scatter | solution.py:76
  427.4 52.9 %all_gather.20 = f32[8,8192]{1,0:T(8,128)S(1)} all-gather(f32[8,512]{1,0:T(8,128)} %reduce-scatter.9.cloned.1.call-done), channel_id=1, replica_groups=mesh['leaf'=32,'col'=16] {'col'}, dimensions={1}, use_global_device_ids=true | all-gather | bytes 278528 | tf_op jit(solution)/shard_map/all_gather | solution.py:66
  480.3 32.5 %all_to_all.77 = f32[8,32,256]{2,0,1:T(8,128)S(1)} all-to-all(f32[8,32,256]{2,0,1:T(8,128)S(1)} %bitcast.192), channel_id=1, replica_groups=mesh['leaf'=32,'col'=16] {'leaf'}, dimensions={1} | all-to-all | bytes 524288 | tf_op jit(solution)/shard_map/all_to_all | solution.py:67
  512.7 0.3 all_to_all.63
  513.0 0.4 slice_subtract_fusion.1
  513.4 1.4 fusion.8
  514.9 121.2 %reduce-scatter.11.cloned.1.call-done = f32[8,512]{1,0:T(8,128)} async-done(((f32[256,512]{1,0:T(8,128)}), f32[8,512]{1,0:T(8,128)}) %reduce-scatter.11.cloned.1.call-update) | async-done | bytes 16400 | tf_op jit(solution)/shard_map/reduce_scatter | solution.py:76
  636.1 1.3 pad_maximum_fusion
  637.5 81.3 %all-gather.2.cloned.1.call-done = f32[256,2,512]{2,0,1:T(8,128)} async-done(((f32[8,2,512]{2,0,1:T(8,128)}), f32[256,2,512]{2,0,1:T(8,128)}) %all-gather.2.cloned.1.call-update) | async-done | bytes 1048592 | tf_op jit(solution)/shard_map/all_gather | solution.py:62
  718.8 2.4 fusion.3
  721.3 113.1 %reduce-scatter.13.cloned.1.call-done = f32[16,256]{1,0:T(8,128)} async-done(((f32[256,256]{1,0:T(8,128)}), f32[16,256]{1,0:T(8,128)}) %reduce-scatter.13.cloned.1.call-update) | async-done | bytes 16400 | tf_op jit(solution)/shard_map/reduce_scatter | solution.py:87
  834.3 36.0 %all_gather.22 = f32[16,8192]{1,0:T(8,128)S(1)} all-gather(f32[16,256]{1,0:T(8,128)} %reduce-scatter.13.cloned.1.call-done), channel_id=1, replica_groups=mesh['leaf'=32,'col'=16] {'leaf'}, dimensions={1}, use_global_device_ids=true | all-gather | bytes 540672 | tf_op jit(solution)/shard_map/all_gather | solution.py:71
  870.4 41.3 %all_to_all.78 = f32[16,16,512]{2,0,1:T(8,128)S(1)} all-to-all(f32[16,16,512]{2,0,1:T(8,128)S(1)} %bitcast.187), channel_id=1, replica_groups=mesh['leaf'=32,'col'=16] {'col'}, dimensions={1} | all-to-all | bytes 1048576 | tf_op jit(solution)/shard_map/all_to_all | solution.py:72
  911.7 1.3 fusion.53
  913.1 106.2 %reduce-scatter.15.cloned.1.call-done = f32[16,256]{1,0:T(8,128)} async-done(((f32[256,256]{1,0:T(8,128)}), f32[16,256]{1,0:T(8,128)}) %reduce-scatter.15.cloned.1.call-update) | async-done | bytes 16400 | tf_op jit(solution)/shard_map/reduce_scatter | solution.py:87
  1019.3 36.1 %all_gather.23 = f32[16,8192]{1,0:T(8,128)S(1)} all-gather(f32[16,256]{1,0:T(8,128)} %reduce-scatter.15.cloned.1.call-done), channel_id=1, replica_groups=mesh['leaf'=32,'col'=16] {'leaf'}, dimensions={1}, use_global_device_ids=true | all-gather | bytes 540672 | tf_op jit(solution)/shard_map/all_gather | solution.py:71
  1055.4 41.4 %all_to_all.79 = f32[16,16,512]{2,0,1:T(8,128)S(1)} all-to-all(f32[16,16,512]{2,0,1:T(8,128)S(1)} %bitcast.190), channel_id=1, replica_groups=mesh['leaf'=32,'col'=16] {'col'}, dimensions={1} | all-to-all | bytes 1048576 | tf_op jit(solution)/shard_map/all_to_all | solution.py:72
  1096.8 1.3 fusion.5
  1098.2 0.6 copy_bitcast_fusion.4
  1098.8 0.6 copy_bitcast_fusion.2
  1099.4 105.0 %reduce-scatter.17.cloned.1.call-done = f32[16,256]{1,0:T(8,128)} async-done(((f32[256,256]{1,0:T(8,128)}), f32[16,256]{1,0:T(8,128)}) %reduce-scatter.17.cloned.1.call-update) | async-done | bytes 16400 | tf_op jit(solution)/shard_map/reduce_scatter | solution.py:87
  1204.4 0.7 pad_maximum_fusion.1
  1205.1 0.6 copy.83
  (82 shorter events, 1.0 us)
Async XLA Ops:
  7.2 5.7 copy-start
  7.2 212.1 %reduce-scatter.7.cloned.1.call-start = ((), (), s32[]{:S(2)}) async-start(), calls=%async_computation.10 | async-start | bytes 540672 | tf_op jit(solution)/shard_map/reduce_scatter | solution.py:76
  7.2 0.7 copy-start.11
  7.2 1.3 copy-start.12
  8.6 0.9 slice-start
  9.5 2.1 copy-start.6
  13.9 1.9 copy-start.15
  13.9 5.6 collective-permute-start
  15.8 0.7 copy-start.16
  16.5 0.7 copy-start.17
  18.7 0.7 copy-start.13
  19.5 1.9 copy-start.4
  20.1 1.0 copy-start.7
  21.4 4.8 copy-start.14
  22.0 8.1 copy-start.5
  22.4 5.9 collective-permute-start.1
  28.8 1.0 copy-start.8
  30.1 64.5 %copy-start.1 = (f32[2,256,512]{2,1,0:T(8,128)S(1)}, f32[2,256,512]{2,1,0:T(8,128)}, u32[]{:S(2)}) copy-start(f32[2,256,512]{2,1,0:T(8,128)} %param.30) | copy-start | bytes 3145732
  96.1 208.7 %copy-start.2 = (f32[256,512]{1,0:T(8,128)S(1)}, f32[256,512]{1,0:T(8,128)}, u32[]{:S(2)}) copy-start(f32[256,512]{1,0:T(8,128)} %param.31) | copy-start | bytes 1572868
  96.1 331.2 %reduce-scatter.9.cloned.1.call-start = ((), (), s32[]{:S(2)}) async-start(), calls=%async_computation.11 | async-start | bytes 540672 | tf_op jit(solution)/shard_map/reduce_scatter | solution.py:76
  306.3 329.9 %reduce-scatter.11.cloned.1.call-start = ((), (), s32[]{:S(2)}) async-start(), calls=%async_computation.12 | async-start | bytes 540672 | tf_op jit(solution)/shard_map/reduce_scatter | solution.py:76
  514.8 121.3 %copy-start.10 = (f32[8,512]{1,0:T(8,128)S(1)}, f32[8,512]{1,0:T(8,128)}, u32[]{:S(2)}) copy-start(f32[8,512]{1,0:T(8,128)} %reduce-scatter.7.cloned.1.call-done) | copy-start | bytes 49156
  514.9 204.0 %all-gather.2.cloned.1.call-start = ((), (), s32[]{:S(2)}) async-start(), calls=%async_computation.13 | async-start | bytes 1081344 | tf_op jit(solution)/shard_map/all_gather | solution.py:62
  637.5 196.9 %reduce-scatter.13.cloned.1.call-start = ((), (), s32[]{:S(2)}) async-start(), calls=%async_computation.14 | async-start | bytes 278528 | tf_op jit(solution)/shard_map/reduce_scatter | solution.py:87
  721.2 298.1 %reduce-scatter.15.cloned.1.call-start = ((), (), s32[]{:S(2)}) async-start(), calls=%async_computation.15 | async-start | bytes 278528 | tf_op jit(solution)/shard_map/reduce_scatter | solution.py:87
  913.0 291.4 %reduce-scatter.17.cloned.1.call-start = ((), (), s32[]{:S(2)}) async-start(), calls=%async_computation.16 | async-start | bytes 278528 | tf_op jit(solution)/shard_map/reduce_scatter | solution.py:87
  1055.4 41.4 %copy-start.3 = (f32[256,2,512]{2,0,1:T(8,128)S(1)}, f32[256,2,512]{2,0,1:T(8,128)}, u32[]{:S(2)}) copy-start(f32[256,2,512]{2,0,1:T(8,128)} %all-gather.2.cloned.1.call-done) | copy-start | bytes 3145732
  1098.8 105.6 %copy-start.9 = (f32[16,256]{1,0:T(8,128)S(1)}, f32[16,256]{1,0:T(8,128)}, u32[]{:S(2)}) copy-start(f32[16,256]{1,0:T(8,128)} %reduce-scatter.13.cloned.1.call-done) | copy-start | bytes 49156
Sparse Core Ops, SparseCore 0:
  96.2 122.9 reduce-scatter.6
  306.4 120.9 reduce-scatter.8
  515.0 121.0 reduce-scatter.10
  638.9 79.8 all-gather.1
  723.2 111.0 reduce-scatter.12
  913.2 106.0 reduce-scatter.14
  1098.3 106.0 reduce-scatter.16
where the time goes:
time: 1210 us
  waiting for transfers between devices  773 us (64%)
  blocking collectives  389 us (32%)
  between operations  14.6 us (1%)
  matrix products  13.9 us (1%)
    reduce_scatter x3, waiting for transfers between devices, forward_product(): lax.psum_scatter(jnp.dot(values, matrix, precision=lax.Precision.HIGHEST,...  365 us
    reduce_scatter x3, waiting for transfers between devices, backward_product(): lax.psum_scatter(lax.dot_general(values, matrix, (((1,), (1,)), ((), ()))...  324 us
    all_gather x2, blocking collectives, to_leaf_rows(): full_rows = lax.all_gather(values, 'col', axis=1, tiled=True)  106 us
    all_to_all x2, blocking collectives, to_column_rows(): lax.all_to_all(full_rows, 'col', split_axis=1, concat_axis=0, tiled=True)  82.7 us
    all_gather x1, waiting for transfers between devices, spread_leaf(): return lax.all_gather(values, 'leaf', axis=0, tiled=True)  81.3 us
    all_gather x2, blocking collectives, to_column_rows(): full_rows = lax.all_gather(values, 'leaf', axis=1, tiled=True)  72.1 us
    all_to_all x2, blocking collectives, to_leaf_rows(): lax.all_to_all(full_rows, 'leaf', split_axis=1, concat_axis=0, tiled=True)  64.9 us
    all_gather x1, blocking collectives, spread_columns(): return lax.all_gather(values, 'col', axis=0, tiled=True)  62.8 us
  transfers between devices with their start and end apart: 9, of which 8 were waited for; matrix products, arithmetic and copies ran while one was open for 0% of the time, Pallas kernels for 0%

commit v1 on v0

--- a/solution.py
+++ b/solution.py
@@ -69,7 +69,10 @@
 
 def to_column_rows(values):
     full_rows = lax.all_gather(values, "leaf", axis=1, tiled=True)
-    return lax.all_to_all(full_rows, "col", split_axis=1, concat_axis=0, tiled=True)
+    return jnp.concatenate(
+        lax.all_to_all(jnp.stack(jnp.split(full_rows, lax.axis_size("col"), axis=1)), "col", 0, 0),
+        axis=0,
+    )
 
 
 def forward_product(values, matrix):

time: 1210 us -> 1210 us (level)
  no operation moved by 1% of the time
where the time goes in v1:
time: 1210 us
  waiting for transfers between devices  773 us (64%)
  blocking collectives  389 us (32%)
  between operations  14.8 us (1%)
  matrix products  13.9 us (1%)
    reduce_scatter x3, waiting for transfers between devices, forward_product(): lax.psum_scatter(jnp.dot(values, matrix, precision=lax.Precision.HIGHEST,...  365 us
    reduce_scatter x3, waiting for transfers between devices, backward_product(): lax.psum_scatter(lax.dot_general(values, matrix, (((1,), (1,)), ((), ()))...  324 us
    all_gather x2, blocking collectives, to_leaf_rows(): full_rows = lax.all_gather(values, 'col', axis=1, tiled=True)  106 us
    all_to_all x2, blocking collectives, to_column_rows(): lax.all_to_all(jnp.stack(jnp.split(full_rows, lax.axis_size('col'), axis=...  82.7 us
    all_gather x1, waiting for transfers between devices, spread_leaf(): return lax.all_gather(values, 'leaf', axis=0, tiled=True)  81.3 us
    all_gather x2, blocking collectives, to_column_rows(): full_rows = lax.all_gather(values, 'leaf', axis=1, tiled=True)  72.1 us
    all_to_all x2, blocking collectives, to_leaf_rows(): lax.all_to_all(full_rows, 'leaf', split_axis=1, concat_axis=0, tiled=True)  64.9 us
    all_gather x1, blocking collectives, spread_columns(): return lax.all_gather(values, 'col', axis=0, tiled=True)  62.8 us
  transfers between devices with their start and end apart: 9, of which 8 were waited for; matrix products, arithmetic and copies ran while one was open for 0% of the time, Pallas kernels for 0%

profile of v1, /device:TPU:2, one launch (start us, length us, event | category | flops | bytes accessed | tf_op | source)
XLA Modules:
  0.0 1212.9 jit_solution(6717064641563398963)
XLA Ops:
  7.3 0.7 copy-done.11
  8.0 0.6 fusion.52
  8.5 0.1 copy.60
  8.6 0.9 slice-done
  9.6 2.0 fusion.47
  11.6 1.3 convolution_multiply_fusion.2
  12.9 0.6 convolution_bitcast_fusion.3
  13.5 0.3 fusion
  13.9 1.9 collective-permute-start
  15.8 0.6 copy-done.16
  16.5 0.6 copy-done.17
  17.1 0.5 broadcast.169
  17.6 0.7 reduce.3
  18.3 0.1 squeeze.47
  18.4 0.1 broadcast_bitcast_fusion.1
  18.5 0.1 broadcast_bitcast_fusion.2
  18.6 0.1 broadcast_bitcast_fusion
  18.7 0.7 copy-done.13
  19.3 0.1 copy.66
  19.5 0.6 gather_fusion
  20.2 0.8 copy-done.7
  21.1 0.3 convolution_multiply_fusion.1
  21.4 0.6 convolution_bitcast_fusion.2
  22.0 0.3 fusion.1
  22.4 3.8 collective-permute-start.1
  26.2 0.1 copy.72
  26.3 1.9 collective-permute-done.1
  28.3 0.6 gather_fusion.1
  29.0 0.8 copy-done.8
  29.8 0.3 convolution_multiply_fusion
  30.1 0.6 convolution_bitcast_fusion.1
  30.7 0.3 fusion.2
  31.0 0.6 gather_fusion.2
  31.6 62.8 %all_gather.18 = f32[256,2,256]{2,1,0:T(2,128)S(1)} all-gather(f32[16,2,256]{2,1,0:T(2,128)S(1)} %broadcast_select_fusion), channel_id=1, replica_groups=mesh['leaf'=32,'col'=16] {'col'}, dimensions={0}, use_global_device_ids=true | all-gather | bytes 557056 | tf_op jit(solution)/shard_map/all_gather | solution.py:58
  94.5 0.2 slice.72
  94.7 1.4 fusion.11
  96.2 123.1 %reduce-scatter.7.cloned.1.call-done = f32[8,512]{1,0:T(8,128)} async-done(((f32[256,512]{1,0:T(8,128)}), f32[8,512]{1,0:T(8,128)}) %reduce-scatter.7.cloned.1.call-update) | async-done | bytes 16400 | tf_op jit(solution)/shard_map/reduce_scatter | solution.py:79
  219.2 53.1 %all_gather.19 = f32[8,8192]{1,0:T(8,128)S(1)} all-gather(f32[8,512]{1,0:T(8,128)} %reduce-scatter.7.cloned.1.call-done), channel_id=1, replica_groups=mesh['leaf'=32,'col'=16] {'col'}, dimensions={1}, use_global_device_ids=true | all-gather | bytes 278528 | tf_op jit(solution)/shard_map/all_gather | solution.py:66
  272.4 32.4 %all_to_all.48 = f32[8,32,256]{2,0,1:T(8,128)S(1)} all-to-all(f32[8,32,256]{2,0,1:T(8,128)S(1)} %bitcast.306), channel_id=1, replica_groups=mesh['leaf'=32,'col'=16] {'leaf'}, dimensions={1} | all-to-all | bytes 524288 | tf_op jit(solution)/shard_map/all_to_all | solution.py:67
  304.8 1.4 fusion.21
  306.3 0.0 reduce-scatter.11.cloned.1.call-start
  306.3 121.1 %reduce-scatter.9.cloned.1.call-done = f32[8,512]{1,0:T(8,128)} async-done(((f32[256,512]{1,0:T(8,128)}), f32[8,512]{1,0:T(8,128)}) %reduce-scatter.9.cloned.1.call-update) | async-done | bytes 16400 | tf_op jit(solution)/shard_map/reduce_scatter | solution.py:79
  427.4 52.9 %all_gather.20 = f32[8,8192]{1,0:T(8,128)S(1)} all-gather(f32[8,512]{1,0:T(8,128)} %reduce-scatter.9.cloned.1.call-done), channel_id=1, replica_groups=mesh['leaf'=32,'col'=16] {'col'}, dimensions={1}, use_global_device_ids=true | all-gather | bytes 278528 | tf_op jit(solution)/shard_map/all_gather | solution.py:66
  480.3 32.5 %all_to_all.49 = f32[8,32,256]{2,0,1:T(8,128)S(1)} all-to-all(f32[8,32,256]{2,0,1:T(8,128)S(1)} %bitcast.304), channel_id=1, replica_groups=mesh['leaf'=32,'col'=16] {'leaf'}, dimensions={1} | all-to-all | bytes 524288 | tf_op jit(solution)/shard_map/all_to_all | solution.py:67
  512.7 0.3 all_to_all.41
  513.0 0.4 slice_subtract_fusion.1
  513.4 1.4 fusion.8
  514.9 121.2 %reduce-scatter.11.cloned.1.call-done = f32[8,512]{1,0:T(8,128)} async-done(((f32[256,512]{1,0:T(8,128)}), f32[8,512]{1,0:T(8,128)}) %reduce-scatter.11.cloned.1.call-update) | async-done | bytes 16400 | tf_op jit(solution)/shard_map/reduce_scatter | solution.py:79
  636.1 1.3 pad_maximum_fusion
  637.5 81.3 %all-gather.2.cloned.1.call-done = f32[256,2,512]{2,0,1:T(8,128)} async-done(((f32[8,2,512]{2,0,1:T(8,128)}), f32[256,2,512]{2,0,1:T(8,128)}) %all-gather.2.cloned.1.call-update) | async-done | bytes 1048592 | tf_op jit(solution)/shard_map/all_gather | solution.py:62
  718.8 2.4 fusion.3
  721.3 113.1 %reduce-scatter.13.cloned.1.call-done = f32[16,256]{1,0:T(8,128)} async-done(((f32[256,256]{1,0:T(8,128)}), f32[16,256]{1,0:T(8,128)}) %reduce-scatter.13.cloned.1.call-update) | async-done | bytes 16400 | tf_op jit(solution)/shard_map/reduce_scatter | solution.py:90
  834.3 36.0 %all_gather.22 = f32[16,8192]{1,0:T(8,128)S(1)} all-gather(f32[16,256]{1,0:T(8,128)} %reduce-scatter.13.cloned.1.call-done), channel_id=1, replica_groups=mesh['leaf'=32,'col'=16] {'leaf'}, dimensions={1}, use_global_device_ids=true | all-gather | bytes 540672 | tf_op jit(solution)/shard_map/all_gather | solution.py:71
  870.6 41.3 %all_to_all.50 = f32[16,16,512]{2,1,0:T(8,128)S(1)} all-to-all(f32[16,16,512]{2,1,0:T(8,128)S(1)} %constant_dynamic-update-slice_fusion), channel_id=1, replica_groups=mesh['leaf'=32,'col'=16] {'col'}, dimensions={0} | all-to-all | bytes 1048576 | tf_op jit(solution)/shard_map/all_to_all | solution.py:73
  911.8 1.3 fusion.53
  913.2 106.2 %reduce-scatter.15.cloned.1.call-done = f32[16,256]{1,0:T(8,128)} async-done(((f32[256,256]{1,0:T(8,128)}), f32[16,256]{1,0:T(8,128)}) %reduce-scatter.15.cloned.1.call-update) | async-done | bytes 16400 | tf_op jit(solution)/shard_map/reduce_scatter | solution.py:90
  1019.4 36.1 %all_gather.23 = f32[16,8192]{1,0:T(8,128)S(1)} all-gather(f32[16,256]{1,0:T(8,128)} %reduce-scatter.15.cloned.1.call-done), channel_id=1, replica_groups=mesh['leaf'=32,'col'=16] {'leaf'}, dimensions={1}, use_global_device_ids=true | all-gather | bytes 540672 | tf_op jit(solution)/shard_map/all_gather | solution.py:71
  1055.7 41.4 %all_to_all.51 = f32[16,16,512]{2,1,0:T(8,128)S(1)} all-to-all(f32[16,16,512]{2,1,0:T(8,128)S(1)} %constant_dynamic-update-slice_fusion.16), channel_id=1, replica_groups=mesh['leaf'=32,'col'=16] {'col'}, dimensions={0} | all-to-all | bytes 1048576 | tf_op jit(solution)/shard_map/all_to_all | solution.py:73
  1097.1 1.3 fusion.5
  1098.5 0.6 copy_bitcast_fusion.2
  1099.1 0.6 copy_bitcast_fusion
  1099.7 105.0 %reduce-scatter.17.cloned.1.call-done = f32[16,256]{1,0:T(8,128)} async-done(((f32[256,256]{1,0:T(8,128)}), f32[16,256]{1,0:T(8,128)}) %reduce-scatter.17.cloned.1.call-update) | async-done | bytes 16400 | tf_op jit(solution)/shard_map/reduce_scatter | solution.py:90
  1204.7 0.7 pad_maximum_fusion.1
  1205.5 0.6 copy.76
  (112 shorter events, 1.0 us)
Async XLA Ops:
  7.2 5.7 copy-start
  7.2 212.1 %reduce-scatter.7.cloned.1.call-start = ((), (), s32[]{:S(2)}) async-start(), calls=%async_computation.10 | async-start | bytes 540672 | tf_op jit(solution)/shard_map/reduce_scatter | solution.py:79
  7.2 0.7 copy-start.11
  7.2 1.3 copy-start.12
  8.6 0.9 slice-start
  9.5 2.1 copy-start.6
  13.9 1.9 copy-start.15
  13.9 5.6 collective-permute-start
  15.8 0.7 copy-start.16
  16.5 0.7 copy-start.17
  18.7 0.7 copy-start.13
  19.5 1.9 copy-start.4
  20.1 1.0 copy-start.7
  21.4 4.8 copy-start.14
  22.0 8.1 copy-start.5
  22.4 5.9 collective-permute-start.1
  28.8 1.0 copy-start.8
  30.1 64.5 %copy-start.1 = (f32[2,256,512]{2,1,0:T(8,128)S(1)}, f32[2,256,512]{2,1,0:T(8,128)}, u32[]{:S(2)}) copy-start(f32[2,256,512]{2,1,0:T(8,128)} %param.30) | copy-start | bytes 3145732
  96.1 208.7 %copy-start.2 = (f32[256,512]{1,0:T(8,128)S(1)}, f32[256,512]{1,0:T(8,128)}, u32[]{:S(2)}) copy-start(f32[256,512]{1,0:T(8,128)} %param.31) | copy-start | bytes 1572868
  96.1 331.2 %reduce-scatter.9.cloned.1.call-start = ((), (), s32[]{:S(2)}) async-start(), calls=%async_computation.11 | async-start | bytes 540672 | tf_op jit(solution)/shard_map/reduce_scatter | solution.py:79
  306.3 329.9 %reduce-scatter.11.cloned.1.call-start = ((), (), s32[]{:S(2)}) async-start(), calls=%async_computation.12 | async-start | bytes 540672 | tf_op jit(solution)/shard_map/reduce_scatter | solution.py:79
  514.8 121.3 %copy-start.10 = (f32[8,512]{1,0:T(8,128)S(1)}, f32[8,512]{1,0:T(8,128)}, u32[]{:S(2)}) copy-start(f32[8,512]{1,0:T(8,128)} %reduce-scatter.7.cloned.1.call-done) | copy-start | bytes 49156
  514.9 204.0 %all-gather.2.cloned.1.call-start = ((), (), s32[]{:S(2)}) async-start(), calls=%async_computation.13 | async-start | bytes 1081344 | tf_op jit(solution)/shard_map/all_gather | solution.py:62
  637.5 196.9 %reduce-scatter.13.cloned.1.call-start = ((), (), s32[]{:S(2)}) async-start(), calls=%async_computation.14 | async-start | bytes 278528 | tf_op jit(solution)/shard_map/reduce_scatter | solution.py:90
  721.2 298.2 %reduce-scatter.15.cloned.1.call-start = ((), (), s32[]{:S(2)}) async-start(), calls=%async_computation.15 | async-start | bytes 278528 | tf_op jit(solution)/shard_map/reduce_scatter | solution.py:90
  913.2 291.5 %reduce-scatter.17.cloned.1.call-start = ((), (), s32[]{:S(2)}) async-start(), calls=%async_computation.16 | async-start | bytes 278528 | tf_op jit(solution)/shard_map/reduce_scatter | solution.py:90
  1055.5 41.6 %copy-start.3 = (f32[256,2,512]{2,0,1:T(8,128)S(1)}, f32[256,2,512]{2,0,1:T(8,128)}, u32[]{:S(2)}) copy-start(f32[256,2,512]{2,0,1:T(8,128)} %all-gather.2.cloned.1.call-done) | copy-start | bytes 3145732
  1099.1 105.6 %copy-start.9 = (f32[16,256]{1,0:T(8,128)S(1)}, f32[16,256]{1,0:T(8,128)}, u32[]{:S(2)}) copy-start(f32[16,256]{1,0:T(8,128)} %reduce-scatter.13.cloned.1.call-done) | copy-start | bytes 49156
Sparse Core Ops, SparseCore 0:
  96.2 122.9 reduce-scatter.6
  306.4 120.9 reduce-scatter.8
  515.0 121.0 reduce-scatter.10
  638.9 79.8 all-gather.1
  723.2 111.0 reduce-scatter.12
  913.3 106.0 reduce-scatter.14
  1098.6 106.0 reduce-scatter.16
